TPU v7x, 32 devices: a whole 2x2x4 slice. The times are simulated.
32 devices in a mesh: blocks: 8 (over z, core), lev: 4 (over y, x).
Axes of the slice: x: 2, y: 2, z: 4, core: 2. Of those that a mesh axis runs over, the one named last changes fastest.
Arguments:
- tracers: float32 [8, 4, 8, 128, 128], P('blocks', 'lev'), may hold values from -6 to 6
- east_velocity: float32 [8, 8, 128, 128], P('blocks'), may hold values from -0.24 to 0.24
- north_velocity: float32 [8, 8, 128, 128], P('blocks'), may hold values from -0.24 to 0.24
- upward_velocity: float32 [8, 8, 128, 128], P('blocks'), may hold values from -0.24 to 0.24
- target: float32 [8, 4, 8, 128, 128], P('blocks', 'lev'), may hold values from 0.09375 to 12.65625
- bottom: int32 [8, 128, 128], P('blocks'), may hold values from 0 to 8, as said below
- shave_fraction: float32 [8, 128, 128], P('blocks'), may hold values from 0.05 to 1, as said below
- side_bottom: int32 [8, 4, 128], P('blocks'), may hold values from 0 to 8, as said below
- neighbors: int32 [8, 4], P('blocks'), may hold values from -1 to 7, as said below
- fold_partner: int32 [8], P('blocks'), may hold values from -1 to 7, as said below
- thin_pairs: int32 [8, 2, 128], P('blocks'), may hold values from 0 to 16383, as said below
Outputs:
- new_tracers: float32 [8, 4, 8, 128, 128], P('blocks', 'lev')
Inputs may be any that keep to these rules, and one draw needn't show every extreme that they name: The blocks form a grid of 3 block columns, periodic from west to east, and 4 block rows; entries are mutual: neighbors[b,0] = c exactly when neighbors[c,1] = b, and neighbors[b,2] = c exactly when neighbors[c,3] = b; a block's entries that are not -1 differ; blocks of the top row have -1 to the north. `fold_partner`: set exactly for the blocks of the top row; mutual, a block may be its own partner. `bottom`: every block has wet columns. `side_bottom`: equals the bottom of the adjacent column or row of the neighbouring block, across the north fold the partner's top row in reversed order, 0 where no block lies. `thin_pairs`: thin cells of a block are distinct and have bottom 1 or more; each partner is the cell just east of its thin cell in the same row, with a bottom no smaller; no cell appears twice in a block. `shave_fraction`: listed thin cells have 0.05 to 0.2, all other cells 0.5 to 1.
All inputs are finite; a program needn't handle non-finite values.
Results may differ from a plain program's by a relative error of at most 0.0003.
Values sent between devices are 32-bit elements; how exact they have to be, the bound alone decides.
A program may use at most 64 MiB of HBM per device.

v0:
```python
import jax
import jax.numpy as jnp
from jax import lax
from jax.sharding import PartitionSpec as P

RATE = 0.5
facing_order = (1, 0, 3, 2)


def upwind(face, first, second):
    return jnp.maximum(face, 0.0) * first + jnp.minimum(face, 0.0) * second


def column_masks(levels, bottom, shave_fraction):
    level_grid = levels[None, None, :, None, None]
    column_bottom = bottom[:, None, None]
    wet = level_grid < column_bottom
    thick = jnp.where(
        level_grid < column_bottom - 1,
        1.0,
        jnp.where(level_grid == column_bottom - 1, shave_fraction[:, None, None], 0.0),
    )
    return (wet, thick)


def level_pair(field):
    zero_level = jnp.zeros_like(field[:, :, :1])
    return (
        jnp.concatenate([zero_level, field[:, :, :-1]], 2),
        jnp.concatenate([field[:, :, 1:], zero_level], 2),
    )


def advected_field(
    tracers,
    east_flow,
    north_flow,
    upward_flow,
    levels,
    bottom,
    wet,
    thick,
    side_bottom,
    west_pair,
    east_pair,
    south_pair,
    north_pair,
):
    level_grid = levels[None, None, :, None, None]
    column_bottom = bottom[:, None, None]
    edge_levels = levels[None, None, :, None]
    wet_west = edge_levels < side_bottom[:, 0][:, None, None, :]
    wet_east = edge_levels < side_bottom[:, 1][:, None, None, :]
    wet_south = edge_levels < side_bottom[:, 2][:, None, None, :]
    wet_north = edge_levels < side_bottom[:, 3][:, None, None, :]
    east_values = jnp.concatenate([tracers[..., 1:], east_pair[0][..., None]], -1)
    east_flows = jnp.concatenate([east_flow[..., 1:], east_pair[1][..., None]], -1)
    east_wets = jnp.concatenate([wet[..., 1:], wet_east[..., None]], -1)
    flux_east = upwind(
        jnp.where(wet & east_wets, 0.5 * (east_flow + east_flows), 0.0), tracers, east_values
    )
    west_face = jnp.where(wet_west & wet[..., 0], 0.5 * (west_pair[1] + east_flow[..., 0]), 0.0)
    flux_west = jnp.concatenate(
        [upwind(west_face, west_pair[0], tracers[..., 0])[..., None], flux_east[..., :-1]], -1
    )
    north_values = jnp.concatenate([tracers[..., 1:, :], north_pair[0][..., None, :]], -2)
    north_flows = jnp.concatenate([north_flow[..., 1:, :], north_pair[1][..., None, :]], -2)
    north_wets = jnp.concatenate([wet[..., 1:, :], wet_north[..., None, :]], -2)
    flux_north = upwind(
        jnp.where(wet & north_wets, 0.5 * (north_flow + north_flows), 0.0), tracers, north_values
    )
    south_face = jnp.where(
        wet_south & wet[..., 0, :], 0.5 * (south_pair[1] + north_flow[..., 0, :]), 0.0
    )
    flux_south = jnp.concatenate(
        [
            upwind(south_face, south_pair[0], tracers[..., 0, :])[..., None, :],
            flux_north[..., :-1, :],
        ],
        -2,
    )
    above_values, below_values = level_pair(tracers)
    above_flow, below_flow = level_pair(upward_flow)
    wet_above = (level_grid >= 1) & (level_grid - 1 < column_bottom)
    wet_below = level_grid + 1 < column_bottom
    flux_lower = upwind(
        jnp.where(wet & wet_below, 0.5 * (upward_flow + below_flow), 0.0), below_values, tracers
    )
    flux_upper = upwind(
        jnp.where(wet & wet_above, 0.5 * (above_flow + upward_flow), 0.0), tracers, above_values
    )
    divergence = flux_west - flux_east + flux_south - flux_north + flux_lower - flux_upper
    return tracers + jnp.where(wet, divergence / jnp.where(wet, thick, 1.0), 0.0)


def merge_block(field, bottom, shave_fraction, pairs, levels):
    flat = field.reshape(field.shape[0], field.shape[1], -1)
    thin_cells = pairs[0]
    partner = pairs[1]
    depth_index = bottom[thin_cells] - 1
    thin_thick = shave_fraction[thin_cells]
    partner_thick = jnp.where(bottom[partner] - 1 == depth_index, shave_fraction[partner], 1.0)
    thin_values = flat[:, :, thin_cells]
    partner_values = flat[:, :, partner]
    merged = (thin_thick * thin_values + partner_thick * partner_values) / (
        thin_thick + partner_thick
    )
    struck = levels[:, None] == depth_index[None, :]
    flat = flat.at[:, :, thin_cells].set(jnp.where(struck, merged, thin_values))
    flat = flat.at[:, :, partner].set(jnp.where(struck, merged, partner_values))
    return flat.reshape(field.shape)


def local(
    tracers,
    east_velocity,
    north_velocity,
    upward_velocity,
    target,
    bottom,
    shave_fraction,
    side_bottom,
    neighbors,
    fold_partner,
    thin_pairs,
):
    blocks_here, tracer_count, level_count, cells_side, _ = tracers.shape
    levels = jnp.arange(level_count, dtype=jnp.int32)
    east_flow = east_velocity[:, None]
    north_flow = north_velocity[:, None]
    upward_flow = upward_velocity[:, None]
    wet, thick = column_masks(levels, bottom, shave_fraction)
    restoring = RATE * (target - tracers)
    tracer_edges = jnp.stack(
        [
            tracers[..., 0],
            tracers[..., cells_side - 1],
            tracers[..., 0, :],
            tracers[..., cells_side - 1, :],
        ],
        1,
    )
    flow_edges = jnp.stack(
        [
            east_velocity[..., 0],
            east_velocity[..., cells_side - 1],
            north_velocity[..., 0, :],
            north_velocity[..., cells_side - 1, :],
        ],
        1,
    )
    tracer_piece = lax.all_gather(tracer_edges, "blocks", axis=0, tiled=True)
    flow_piece = lax.all_gather(flow_edges, "blocks", axis=0, tiled=True)
    owners = jnp.arange(tracer_piece.shape[0], dtype=jnp.int32)
    side_match = (neighbors[:, :, None] == owners[None, None, :]).astype(jnp.float32)
    fold_match = (fold_partner[:, None] == owners[None, :]).astype(jnp.float32)
    tracer_facing = jnp.stack([tracer_piece[:, side] for side in facing_order], 1)
    flow_facing = jnp.stack([flow_piece[:, side] for side in facing_order], 1)
    highest = lax.Precision.HIGHEST
    tracer_sides = jnp.einsum("bsq,qstlc->bstlc", side_match, tracer_facing, precision=highest)
    flow_sides = jnp.einsum("bsq,qslc->bslc", side_match, flow_facing, precision=highest)
    tracer_fold = jnp.einsum("bq,qtlc->btlc", fold_match, tracer_piece[:, 3], precision=highest)
    flow_fold = jnp.einsum("bq,qlc->blc", fold_match, flow_piece[:, 3], precision=highest)
    tracer_sides, flow_sides, tracer_fold, flow_fold = (
        tracer_sides,
        flow_sides,
        tracer_fold,
        flow_fold,
    )
    west_pair = (tracer_sides[:, 0], flow_sides[:, 0][:, None])
    east_pair = (tracer_sides[:, 1], flow_sides[:, 1][:, None])
    south_pair = (tracer_sides[:, 2], flow_sides[:, 2][:, None])
    north_pair = (
        tracer_sides[:, 3] + tracer_fold[..., ::-1],
        (flow_sides[:, 3] - flow_fold[..., ::-1])[:, None],
    )
    advected = advected_field(
        tracers,
        east_flow,
        north_flow,
        upward_flow,
        levels,
        bottom,
        wet,
        thick,
        side_bottom,
        west_pair,
        east_pair,
        south_pair,
        north_pair,
    )
    source_part = jnp.sum(jnp.where(wet, thick * restoring, 0.0))
    volume_part = tracer_count * jnp.sum(jnp.where(wet, thick, 0.0))
    total_source, total_volume = lax.psum((source_part, volume_part), ("blocks", "lev"))
    stepped = jnp.where(wet, advected + restoring - total_source / total_volume, 0.0)
    return jax.vmap(merge_block, in_axes=(0, 0, 0, 0, None))(
        stepped,
        bottom.reshape(blocks_here, -1),
        shave_fraction.reshape(blocks_here, -1),
        thin_pairs,
        levels,
    )


def solution(mesh):
    placed = (
        P("blocks", "lev", None, None, None),
        P("blocks", None, None, None),
        P("blocks", None, None, None),
        P("blocks", None, None, None),
        P("blocks", "lev", None, None, None),
        P("blocks", None, None),
        P("blocks", None, None),
        P("blocks", None, None),
        P("blocks", None),
        P("blocks"),
        P("blocks", None, None),
    )
    return jax.shard_map(
        local,
        mesh=mesh,
        in_specs=placed,
        out_specs=P("blocks", "lev", None, None, None),
        check_vma=False,
    )
```

profile of v0, /device:TPU:0, one launch (start us, length us, event | category | flops | bytes accessed | tf_op | source)
XLA Modules:
  0.0 142.8 jit_solution(14295205948113703087)
XLA Ops:
  3.4 1.8 %gather_fusion.4 = f32[128]{0:T(128)S(1)} fusion(f32[1,16384]{1,0:T(1,128)} %bitcast.215, s32[128]{0:T(128)S(1)} %get-tuple-element.43), kind=kCustom, calls=%fused_computation.4 | custom fusion | bytes 2048 | tf_op jit(solution)/shard_map/vmap()/gather | solution.py:102
  5.1 1.8 %gather_fusion.3 = s32[128]{0:T(128)S(1)} fusion(s32[1,16384]{1,0:T(1,128)} %bitcast.212, s32[128]{0:T(128)S(1)} %get-tuple-element.43), kind=kCustom, calls=%fused_computation.3 | custom fusion | bytes 2048 | tf_op jit(solution)/shard_map/vmap()/gather | solution.py:102
  7.5 1.8 %gather_fusion.1 = f32[128]{0:T(128)S(1)} fusion(f32[1,16384]{1,0:T(1,128)} %bitcast.216, s32[128]{0:T(128)S(1)} %get-tuple-element.46), kind=kCustom, calls=%fused_computation.1 | custom fusion | bytes 2048 | tf_op jit(solution)/shard_map/vmap()/gather | solution.py:101
  9.2 1.8 %gather_fusion = s32[128]{0:T(128)S(1)} fusion(s32[1,16384]{1,0:T(1,128)} %bitcast.213, s32[128]{0:T(128)S(1)} %get-tuple-element.46), kind=kCustom, calls=%fused_computation | custom fusion | bytes 2048 | tf_op jit(solution)/shard_map/vmap()/gather | solution.py:100
  11.6 1.4 slice_bitcast_fusion.15
  16.0 0.9 copy.235
  20.0 1.3 copy.236
  21.3 15.7 %all_gather.7 = f32[8,4,1,8,128]{4,3,2,1,0:T(8,128)S(1)} all-gather(f32[1,4,1,8,128]{4,3,2,1,0:T(8,128)S(1)} %pad_maximum_fusion.2), channel_id=1, replica_groups=mesh['blocks'=8,'lev'=4] {'blocks'}, dimensions={0}, use_global_device_ids=true | all-gather | bytes 147456 | tf_op jit(solution)/shard_map/all_gather | solution.py:152
  37.6 1.0 copy.227
  39.5 1.3 copy.209
  40.8 14.0 %all_gather.6 = f32[8,4,8,128]{3,2,1,0:T(8,128)S(1)} all-gather(f32[1,4,8,128]{3,2,1,0:T(8,128)S(1)} %pad_maximum_fusion.1), channel_id=1, replica_groups=mesh['blocks'=8,'lev'=4] {'blocks'}, dimensions={0}, use_global_device_ids=true | all-gather | bytes 147456 | tf_op jit(solution)/shard_map/all_gather | solution.py:153
  55.3 1.0 copy.224
  57.6 1.3 copy.221
  59.8 1.0 copy.228
  61.3 4.0 %select_reduce_fusion = (f32[]{:T(128)}, f32[]{:T(128)}, f32[1,1,8,128,128]{3,2,4,1,0:T(8,128)}, f32[1,1,8,128,128]{3,2,4,1,0:T(8,128)S(1)}) fusion(f32[128,128]{0,1:T(8,128)S(1)} %copy.235, s32[128,128]{0,1:T(8,128)S(1)} %copy.234, s32[128,128]{0,1:T(8,128)S(1)} %copy.208, f32[1,1,8,128,128]{3,2,4,1,0:T(8,128)S(1)} %copy.237, ...), kind=kLoop, calls=%fused_computation.28 | loop fusion | flops 4718590 | bytes 5701640 | tf_op jit(solution)/shard_map/reduce_sum | solution.py:193
  65.3 40.5 %all-reduce.4 = (f32[]{:T(128)}, f32[]{:T(128)}) all-reduce(f32[]{:T(128)} %get-tuple-element.6, f32[]{:T(128)} %get-tuple-element.5), channel_id=1, replica_groups=mesh['blocks'=8,'lev'=4] {'blocks','lev'}, use_global_device_ids=true, to_apply=%region_1.2 | all-reduce | flops 2 | bytes 16 | tf_op jit(solution)/shard_map/psum | solution.py:194
  107.1 1.1 slice.225
  108.3 2.3 %subtract_select_fusion = f32[1,1,8,128,128]{3,2,4,1,0:T(8,128)S(1)} fusion(f32[1,1,8,128,128]{3,2,4,1,0:T(8,128)S(1)} %copy.236, f32[1,1,8,128,128]{3,2,4,1,0:T(8,128)S(1)} %get-tuple-element.12, f32[1,1,8,127,128]{3,2,4,1,0:T(8,128)S(1)} %bitcast.223, f32[1,1,8,1,128]{3,2,4,1,0:T(8,128)} %copy.228, f32[1,1,8,128,128]{3,2,4,1,0:T(8,128)} %get-tuple-element.11, ...), kind=kLoop, calls=%fused_computation.27 | loop fusion | flops 5505024 | bytes 6225996 | tf_op jit(solution)/shard_map/jit(_where)/select_n | solution.py:195
  110.6 7.4 %copy.239 = f32[1,1,8,128,128]{2,4,3,1,0:T(8,128)} copy(f32[1,1,8,128,128]{3,2,4,1,0:T(8,128)S(1)} %subtract_select_fusion) | data formatting | bytes 1048576 | tf_op jit(solution)/shard_map/jit(_where)/select_n | solution.py:195
  118.0 1.8 %gather_fusion.5 = f32[128,8]{1,0:T(8,128)S(1)} fusion(f32[1,8,16384]{1,2,0:T(8,128)} %bitcast.208, s32[128]{0:T(128)S(1)} %get-tuple-element.43), kind=kCustom, calls=%fused_computation.5 | custom fusion | bytes 9216 | tf_op jit(solution)/shard_map/vmap()/gather | solution.py:104
  119.8 1.8 %gather_fusion.2 = f32[128,8]{1,0:T(8,128)S(1)} fusion(f32[1,8,16384]{1,2,0:T(8,128)} %bitcast.209, s32[128]{0:T(128)S(1)} %get-tuple-element.46), kind=kCustom, calls=%fused_computation.2 | custom fusion | bytes 9216 | tf_op jit(solution)/shard_map/vmap()/gather | solution.py:103
  121.5 7.7 %scatter_custom_fusion = f32[8,16384]{0,1:T(8,128)} fusion(f32[8,16384]{0,1:T(8,128)} %bitcast.210, s32[128]{0:T(128)} %get-tuple-element.47, f32[128,8]{1,0:T(8,128)S(1)} %gather_fusion.2, f32[128,8]{1,0:T(8,128)S(1)} %gather_fusion.5, f32[128]{0:T(128)S(1)} %gather_fusion.1, s32[128]{0:T(128)S(1)} %broadcast_add_fusion.1, f32[128]{0:T(128)S(1)} %get-tuple-element.9, ...), kind=kCustom, calls=%fused_computation.47 | custom fusion | flops 6144 | bytes 534528 | tf_op jit(solution)/shard_map/vmap()/scatter | solution.py:109
  129.2 7.7 %scatter_custom_fusion.1 = f32[8,16384]{0,1:T(8,128)} fusion(f32[8,16384]{0,1:T(8,128)} %scatter_custom_fusion, s32[128]{0:T(128)} %get-tuple-element.42, f32[128,8]{1,0:T(8,128)S(1)} %gather_fusion.5, f32[128,8]{1,0:T(8,128)S(1)} %gather_fusion.2, f32[128]{0:T(128)S(1)} %gather_fusion.1, s32[128]{0:T(128)S(1)} %broadcast_add_fusion.1, ...), kind=kCustom, calls=%fused_computation.45 | custom fusion | flops 6144 | bytes 534528 | tf_op jit(solution)/shard_map/vmap()/scatter | solution.py:110
  136.9 5.9 %copy.241 = f32[1,1,8,128,128]{4,3,2,1,0:T(8,128)} copy(f32[1,1,8,128,128]{2,4,3,1,0:T(8,128)} %bitcast.211) | data formatting | bytes 1048576 | tf_op jit(solution)/shard_map/vmap()/reshape | solution.py:111
  (51 shorter events, 14.4 us)
Async XLA Ops:
  0.0 57.4 %copy-start.1 = (f32[1,1,8,128,128]{4,3,2,1,0:T(8,128)S(1)}, f32[1,1,8,128,128]{4,3,2,1,0:T(8,128)}, u32[]{:S(2)}) copy-start(f32[1,1,8,128,128]{4,3,2,1,0:T(8,128)} %param.15) | copy-start | bytes 1572868
  0.0 57.1 %copy-start = (f32[1,8,128,128]{3,2,1,0:T(8,128)S(1)}, f32[1,8,128,128]{3,2,1,0:T(8,128)}, u32[]{:S(2)}) copy-start(f32[1,8,128,128]{3,2,1,0:T(8,128)} %param.14) | copy-start | bytes 1572868
where the time goes:
time: 144 us; the launch traced here: 143 us
  blocking collectives  70.2 us (49%)
  local copies, waits for them, and re-layouts  41.9 us (29%)
  other arithmetic  27.6 us (19%)
  between operations  2.28 us (2%)
    psum x1, blocking collectives, local(): lax.psum((source_part, volume_part), ('blocks', 'lev'))  40.5 us
    all_gather x1, blocking collectives, local(): tracer_piece = lax.all_gather(tracer_edges, 'blocks', axis=0, tiled=True)  15.7 us
    all_gather x1, blocking collectives, local(): flow_piece = lax.all_gather(flow_edges, 'blocks', axis=0, tiled=True)  14 us
    scatter x2, other arithmetic, merge_block(): flat = flat.at[:, :, thin_cells].set(jnp.where(struck, merged, thin_values))  8.27 us
    scatter x1, other arithmetic, merge_block(): flat = flat.at[:, :, partner].set(jnp.where(struck, merged, partner_values))  7.68 us
    select_n x1, local copies, waits for them, and re-layouts, local(): jnp.where(wet, advected + restoring - total_source / total_volume, 0.0)  7.4 us
    reshape x1, local copies, waits for them, and re-layouts, merge_block(): return flat.reshape(field.shape)  5.85 us
    unnamed x9, local copies, waits for them, and re-layouts  4.29 us

commit v1 on v0

v1 whole, which is shorter than its diff:
```python
import functools

import jax
import jax.numpy as jnp
from jax import lax
from jax.experimental import pallas as pl
from jax.experimental.pallas import tpu as pltpu
from jax.sharding import PartitionSpec as P

RATE = 0.5
THIN_LIMIT = 0.35
MESH = pl.DeviceIdType.MESH
F32 = jnp.float32
HIGHEST = lax.Precision.HIGHEST


def upwind(face, first, second):
    return jnp.maximum(face, 0.0) * first + jnp.minimum(face, 0.0) * second


def kernel(
    nb,
    nl,
    nbr_ref,
    fold_ref,
    side_ref,
    t_hbm,
    u_hbm,
    v_hbm,
    w_hbm,
    g_hbm,
    bottom_hbm,
    shave_hbm,
    out_ref,
    t_ref,
    u_ref,
    v_ref,
    w_ref,
    g_ref,
    bottom_ref,
    shave_ref,
    x_ref,
    edge_ref,
    pay_ref,
    halo_ref,
    part_ref,
    parts_ref,
    in_sem,
    edge_send,
    edge_recv,
    part_send,
    part_recv,
):
    levels, rows, cols = t_ref.shape
    n = nb * nl
    block = lax.axis_index("blocks")
    lev = lax.axis_index("lev")
    me = block * nl + lev

    loads = [
        pltpu.make_async_copy(src, dst, in_sem.at[i])
        for i, (src, dst) in enumerate(
            (
                (t_hbm, t_ref),
                (u_hbm, u_ref),
                (bottom_hbm, bottom_ref),
                (shave_hbm, shave_ref),
                (g_hbm, g_ref),
                (v_hbm, v_ref),
                (w_hbm, w_ref),
            )
        )
    ]
    for load in loads:
        load.start()

    barrier = pltpu.get_barrier_semaphore()

    def greet(i, carry):
        there = lax.rem(me + i, n)
        pl.semaphore_signal(
            barrier,
            inc=1,
            device_id={"blocks": lax.div(there, nl), "lev": lax.rem(there, nl)},
            device_id_type=MESH,
        )
        return carry

    lax.fori_loop(1, n, greet, 0)

    lane = lax.broadcasted_iota(jnp.int32, (rows, cols), 1)
    row = lax.broadcasted_iota(jnp.int32, (rows, cols), 0)
    lane_pair = lane // 2

    for load in loads[:4]:
        load.wait()
    bottom = bottom_ref[...]
    shave = shave_ref[...]
    strip = jnp.zeros((rows, cols), F32)
    fields = [functools.partial(lambda k: t_ref[k], k) for k in range(levels)]
    fields += [functools.partial(lambda k: u_ref[k], k) for k in range(levels)]
    fields += [lambda: bottom.astype(F32), lambda: shave]
    for j, field in enumerate(fields):
        strip = jnp.where(lane_pair == j, pltpu.roll(field(), 2 * j + 1, 1), strip)
    edge_ref[...] = strip.T

    loads[5].wait()
    t_east = edge_ref[pl.ds(0, levels, stride=2), :]
    t_west = edge_ref[pl.ds(1, levels, stride=2), :]
    u_east = edge_ref[pl.ds(2 * levels, levels, stride=2), :]
    u_west = edge_ref[pl.ds(2 * levels + 1, levels, stride=2), :]
    t_south = t_ref[:, 0, :]
    t_north = t_ref[:, rows - 1, :]
    v_south = v_ref[:, 0, :]
    v_north = v_ref[:, rows - 1, :]
    t_edges = (t_west, t_east, t_south, t_north)
    f_edges = (u_west, u_east, v_south, v_north)
    sides = [nbr_ref[0, s] for s in range(4)]
    fold = fold_ref[0]
    blank = jnp.zeros((levels, cols), F32)

    def compose(there):
        t_side, f_side = blank, blank
        for s in range(4):
            hit = sides[s] == there
            t_side = jnp.where(hit, t_edges[s], t_side)
            f_side = jnp.where(hit, f_edges[s], f_side)
        hit = fold == there
        return t_side, f_side, jnp.where(hit, t_north, blank), jnp.where(hit, v_north, blank)

    def pack(i, carry):
        parts = compose(lax.rem(block + i, nb))
        for p, part in enumerate(parts):
            pay_ref[i - 1, p * levels : (p + 1) * levels, :] = part
        return carry

    lax.fori_loop(1, nb, pack, 0)

    loads[4].wait()
    last = bottom - 1
    source = jnp.zeros((rows, cols), F32)
    for k in range(levels):
        thick = jnp.where(k < last, 1.0, jnp.where(k == last, shave, 0.0))
        source += thick * (RATE * (g_ref[k] - t_ref[k]))
    volume = jnp.where(bottom > 0, last.astype(F32) + shave, 0.0)
    source = jnp.sum(source, axis=0, keepdims=True)
    volume = jnp.sum(volume, axis=0, keepdims=True)
    half = cols // 2
    first_half = lax.broadcasted_iota(jnp.int32, (1, cols), 1) < half
    own_part = jnp.where(
        first_half,
        source + pltpu.roll(source, half, 1),
        volume + pltpu.roll(volume, half, 1),
    )
    part_ref[...] = own_part

    pl.semaphore_wait(barrier, n - 1)

    def send_edges(i, carry):
        pltpu.make_async_remote_copy(
            src_ref=pay_ref.at[i - 1],
            dst_ref=halo_ref.at[i - 1],
            send_sem=edge_send,
            recv_sem=edge_recv,
            device_id={"blocks": lax.rem(block + i, nb), "lev": lev},
            device_id_type=MESH,
        ).start()
        return carry

    def send_part(i, carry):
        there = lax.rem(me + i, n)
        pltpu.make_async_remote_copy(
            src_ref=part_ref,
            dst_ref=parts_ref.at[i - 1],
            send_sem=part_send,
            recv_sem=part_recv,
            device_id={"blocks": lax.div(there, nl), "lev": lax.rem(there, nl)},
            device_id_type=MESH,
        ).start()
        return carry

    lax.fori_loop(1, n, send_part, 0)
    lax.fori_loop(1, nb, send_edges, 0)

    loads[6].wait()
    inverse = 1.0 / shave
    bottom_east = pltpu.roll(bottom, cols - 1, 1)
    open_east = jnp.where(lane == cols - 1, 0, jnp.minimum(bottom, bottom_east))
    open_north = jnp.where(row == rows - 1, 0, jnp.minimum(bottom, pltpu.roll(bottom, rows - 1, 0)))
    upper = jnp.zeros((rows, cols), F32)
    for k in range(levels):
        t = t_ref[k]
        u = u_ref[k]
        v = v_ref[k]
        face = jnp.where(k < open_east, 0.5 * (u + pltpu.roll(u, cols - 1, 1)), 0.0)
        flux = upwind(face, t, pltpu.roll(t, cols - 1, 1))
        divergence = pltpu.roll(flux, 1, 1) - flux
        face = jnp.where(k < open_north, 0.5 * (v + pltpu.roll(v, rows - 1, 0)), 0.0)
        flux = upwind(face, t, pltpu.roll(t, rows - 1, 0))
        divergence += pltpu.roll(flux, 1, 0) - flux
        if k < levels - 1:
            face = jnp.where(k + 1 < bottom, 0.5 * (w_ref[k] + w_ref[k + 1]), 0.0)
            lower = upwind(face, t_ref[k + 1], t)
        else:
            lower = jnp.zeros((rows, cols), F32)
        divergence += lower - upper
        upper = lower
        x_ref[k] = t + divergence * jnp.where(k == last, inverse, 1.0) + RATE * (g_ref[k] - t)

    pltpu.make_async_copy(halo_ref, halo_ref, edge_recv).wait()

    own = compose(block)
    found_t = [jnp.where(sides[s] == block, t_edges[s ^ 1], blank) for s in range(4)]
    found_f = [jnp.where(sides[s] == block, f_edges[s ^ 1], blank) for s in range(4)]

    def collect(i, carry):
        found_t, found_f, fold_t, fold_f = carry
        origin = lax.rem(block + nb - i, nb)
        side_t, side_f, over_t, over_f = (
            halo_ref[i - 1, p * levels : (p + 1) * levels, :] for p in range(4)
        )
        found_t = [jnp.where(sides[s] == origin, side_t, found_t[s]) for s in range(4)]
        found_f = [jnp.where(sides[s] == origin, side_f, found_f[s]) for s in range(4)]
        hit = fold == origin
        return found_t, found_f, jnp.where(hit, over_t, fold_t), jnp.where(hit, over_f, fold_f)

    found_t, found_f, fold_t, fold_f = lax.fori_loop(
        1, nb, collect, (found_t, found_f, own[2], own[3])
    )
    mirror = (
        lax.broadcasted_iota(jnp.int32, (cols, cols), 0)
        + lax.broadcasted_iota(jnp.int32, (cols, cols), 1)
        == cols - 1
    ).astype(F32)
    turned = jnp.dot(
        jnp.concatenate([fold_t, fold_f], 0), mirror, precision=HIGHEST, preferred_element_type=F32
    )
    found_t[3] = found_t[3] + turned[:levels]
    found_f[3] = found_f[3] - turned[levels:]

    grid = lax.broadcasted_iota(jnp.int32, (levels, cols), 0).astype(F32)
    edge_bottom = (
        edge_ref[4 * levels + 1 : 4 * levels + 2, :],
        edge_ref[4 * levels : 4 * levels + 1, :],
        bottom_ref[0:1, :].astype(F32),
        bottom_ref[rows - 1 : rows, :].astype(F32),
    )
    edge_shave = (
        edge_ref[4 * levels + 3 : 4 * levels + 4, :],
        edge_ref[4 * levels + 2 : 4 * levels + 3, :],
        shave_ref[0:1, :],
        shave_ref[rows - 1 : rows, :],
    )
    gains = []
    for s in range(4):
        beyond = side_ref[s : s + 1, :].astype(F32)
        wet = grid < jnp.minimum(edge_bottom[s], beyond)
        face = jnp.where(wet, 0.5 * (f_edges[s] + found_f[s]), 0.0)
        if s % 2 == 0:
            flux = upwind(face, found_t[s], t_edges[s])
        else:
            flux = -upwind(face, t_edges[s], found_t[s])
        gains.append(flux * jnp.where(grid == edge_bottom[s] - 1.0, 1.0 / edge_shave[s], 1.0))
    for k in range(levels):
        x_ref[k, 0:1, :] += gains[2][k : k + 1, :]
        x_ref[k, rows - 1 : rows, :] += gains[3][k : k + 1, :]
    wide = jnp.concatenate(gains[:2], 0)
    place = lax.broadcasted_iota(jnp.int32, (2 * levels, cols), 0)
    place_lane = lax.broadcasted_iota(jnp.int32, (2 * levels, cols), 1)

    partner_shave = jnp.where(bottom_east == bottom, pltpu.roll(shave, cols - 1, 1), 1.0)
    scale = 1.0 / (shave + partner_shave)
    weight = shave * scale
    partner_weight = partner_shave * scale
    struck = jnp.where(shave < THIN_LIMIT, last, -1)
    struck_west = pltpu.roll(struck, 1, 1)

    pltpu.make_async_copy(parts_ref, parts_ref, part_recv).wait()
    total = lax.fori_loop(0, n - 1, lambda i, carry: carry + parts_ref[i], own_part)
    total_source = jnp.sum(jnp.where(first_half, total, 0.0), axis=1, keepdims=True)
    total_volume = jnp.sum(jnp.where(first_half, 0.0, total), axis=1, keepdims=True)
    mean = total_source / total_volume

    for k in range(levels):
        chosen = (place == k) & (place_lane == 0) | (place == levels + k) & (place_lane == cols - 1)
        side_gain = lax.dot_general(
            wide,
            chosen.astype(F32),
            (((0,), (0,)), ((), ())),
            precision=HIGHEST,
            preferred_element_type=F32,
        )
        x = x_ref[k] + side_gain
        merged = weight * x + partner_weight * pltpu.roll(x, cols - 1, 1)
        x = jnp.where(struck == k, merged, x)
        x = jnp.where(struck_west == k, pltpu.roll(merged, 1, 1), x)
        out_ref[k] = jnp.where(k < bottom, x - mean, 0.0)

    pltpu.make_async_copy(halo_ref, halo_ref, edge_send).wait()
    pltpu.make_async_copy(parts_ref, parts_ref, part_send).wait()


def local(
    nb,
    nl,
    tracers,
    east_velocity,
    north_velocity,
    upward_velocity,
    target,
    bottom,
    shave_fraction,
    side_bottom,
    neighbors,
    fold_partner,
    thin_pairs,
):
    levels, rows, cols = tracers.shape[2:]
    cube = (levels, rows, cols)
    n = nb * nl
    smem = pl.BlockSpec(memory_space=pltpu.SMEM)
    vmem = pl.BlockSpec(memory_space=pltpu.VMEM)
    anywhere = pl.BlockSpec(memory_space=pl.ANY)
    stepped = pl.pallas_call(
        functools.partial(kernel, nb, nl),
        out_shape=jax.ShapeDtypeStruct(cube, F32),
        in_specs=[smem, smem, vmem] + [anywhere] * 7,
        out_specs=vmem,
        scratch_shapes=[
            pltpu.VMEM(cube, F32),
            pltpu.VMEM(cube, F32),
            pltpu.VMEM(cube, F32),
            pltpu.VMEM(cube, F32),
            pltpu.VMEM(cube, F32),
            pltpu.VMEM((rows, cols), jnp.int32),
            pltpu.VMEM((rows, cols), F32),
            pltpu.VMEM(cube, F32),
            pltpu.VMEM((cols, rows), F32),
            pltpu.VMEM((nb - 1, 4 * levels, cols), F32),
            pltpu.VMEM((nb - 1, 4 * levels, cols), F32),
            pltpu.VMEM((1, cols), F32),
            pltpu.VMEM((n - 1, 1, cols), F32),
            pltpu.SemaphoreType.DMA((7,)),
            pltpu.SemaphoreType.DMA,
            pltpu.SemaphoreType.DMA,
            pltpu.SemaphoreType.DMA,
            pltpu.SemaphoreType.DMA,
        ],
        compiler_params=pltpu.CompilerParams(collective_id=0, has_side_effects=True),
    )(
        neighbors,
        fold_partner,
        side_bottom.reshape(4, cols),
        tracers.reshape(cube),
        east_velocity.reshape(cube),
        north_velocity.reshape(cube),
        upward_velocity.reshape(cube),
        target.reshape(cube),
        bottom.reshape(rows, cols),
        shave_fraction.reshape(rows, cols),
    )
    return stepped.reshape(tracers.shape)


def solution(mesh):
    placed = (
        P("blocks", "lev", None, None, None),
        P("blocks", None, None, None),
        P("blocks", None, None, None),
        P("blocks", None, None, None),
        P("blocks", "lev", None, None, None),
        P("blocks", None, None),
        P("blocks", None, None),
        P("blocks", None, None),
        P("blocks", None),
        P("blocks"),
        P("blocks", None, None),
    )
    return jax.shard_map(
        functools.partial(local, mesh.shape["blocks"], mesh.shape["lev"]),
        mesh=mesh,
        in_specs=placed,
        out_specs=P("blocks", "lev", None, None, None),
        check_vma=False,
    )
```

time: 144 us -> 16.3 us (0.11)
  blocking collectives: 70.2 us -> 0 us
  local copies, waits for them, and re-layouts: 41.9 us -> 1.87 us
  other arithmetic: 27.6 us -> 0 us
  Pallas kernels: 0 us -> 13.6 us
  between operations: 2.28 us -> 0.66 us
    psum x1 -> x0, blocking collectives: 40.5 us -> none  [local(): lax.psum((source_part, volume_part), ('blocks', 'lev'))]
    all_gather x2 -> x0, blocking collectives: 29.7 us -> none  [the longest x1 15.7 us: local(): tracer_piece = lax.all_gather(tracer_edges, 'blocks', axis=0, tiled=True)]
    scatter x3 -> x0, other arithmetic: 15.9 us -> none  [the longest x2 8.27 us: merge_block(): flat = flat.at[:, :, thin_cells].set(jnp.where(struck, merged, thin_values))]
    pallas_call x0 -> x1, Pallas kernels: none -> 13.6 us  [local(): pl.pallas_call(functools.partial(kernel, nb, nl), out_shape=jax.ShapeDtyp...]
    gather x7 -> x0, local copies, waits for them, and re-layouts: 10.6 us -> none  [the longest x2 1.78 us: merge_block(): bottom[partner] - 1 == depth_index]
    select_n x1 -> x0, local copies, waits for them, and re-layouts: 7.4 us -> none  [local(): jnp.where(wet, advected + restoring - total_source / total_volume, 0.0)]
    slice x14 -> x0, local copies, waits for them, and re-layouts: 6.83 us -> none  [the longest x1 1.08 us: advected_field(): flux_east[..., :-1]]
    reshape x1 -> x0, local copies, waits for them, and re-layouts: 5.85 us -> none  [merge_block(): return flat.reshape(field.shape)]
where the time goes in v1:
time: 16.3 us; the launch traced here: 16.1 us
  Pallas kernels  13.6 us (83%)
  local copies, waits for them, and re-layouts  1.87 us (11%)
  between operations  0.66 us (4%)
    pallas_call x1, Pallas kernels, local(): pl.pallas_call(functools.partial(kernel, nb, nl), out_shape=jax.ShapeDtyp...  13.6 us
    unnamed x1, local copies, waits for them, and re-layouts  1.87 us

profile of v1, /device:TPU:0, one launch (start us, length us, event | category | flops | bytes accessed | tf_op | source)
XLA Modules:
  0.0 16.1 jit_solution(9651058023381409648)
XLA Ops:
  0.7 13.6 %shard_map.100 = f32[8,128,128]{2,1,0:T(8,128)} custom-call(s32[1,4]{1,0:T(1,128)} %nbr_ref.1, s32[1]{0:T(128)S(6)} %copy.12.fold_ref, s32[4,128]{1,0:T(4,128)} %bitcast.17, f32[8,128,128]{2,1,0:T(8,128)} %bitcast.10, f32[8,128,128]{2,1,0:T(8,128)} %bitcast.11, f32[8,128,128]{2,1,0:T(8,128)} %bitcast.12, f32[8,128,128]{2,1,0:T(8,128)} %bitcast.13, ...), custom_call_target="tpu_custom_call" | custom-call | tf_op jit(solution)/shard_map/pallas_call | solution.py:324
  14.3 1.9 %copy.13 = f32[1,1,8,128,128]{4,3,2,1,0:T(8,128)} copy(f32[1,1,8,128,128]{4,3,2,1,0:T(8,128)} %bitcast.9) | data formatting | bytes 1048576

commit v2 on v1

--- a/solution.py
+++ b/solution.py
@@ -21,9 +21,9 @@
 def kernel(
     nb,
     nl,
-    nbr_ref,
-    fold_ref,
-    side_ref,
+    nbr_hbm,
+    fold_hbm,
+    side_hbm,
     t_hbm,
     u_hbm,
     v_hbm,
@@ -39,6 +39,9 @@
     g_ref,
     bottom_ref,
     shave_ref,
+    nbr_ref,
+    fold_ref,
+    side_ref,
     x_ref,
     edge_ref,
     pay_ref,
@@ -53,9 +56,26 @@
 ):
     levels, rows, cols = t_ref.shape
     n = nb * nl
+    unroll = n <= 64
     block = lax.axis_index("blocks")
     lev = lax.axis_index("lev")
-    me = block * nl + lev
+
+    def each_other(visit):
+        def outer(i, carry):
+            there = lax.rem(block + i, nb)
+
+            def inner(j, carry):
+                visit(i * nl + j - 1, {"blocks": there, "lev": lax.rem(lev + j, nl)})
+                return carry
+
+            return lax.fori_loop(0, nl, inner, carry, unroll=unroll)
+
+        def first(j, carry):
+            visit(j - 1, {"blocks": block, "lev": lax.rem(lev + j, nl)})
+            return carry
+
+        lax.fori_loop(1, nb, outer, 0, unroll=unroll)
+        lax.fori_loop(1, nl, first, 0, unroll=unroll)
 
     loads = [
         pltpu.make_async_copy(src, dst, in_sem.at[i])
@@ -68,6 +88,9 @@
                 (g_hbm, g_ref),
                 (v_hbm, v_ref),
                 (w_hbm, w_ref),
+                (nbr_hbm, nbr_ref),
+                (fold_hbm, fold_ref),
+                (side_hbm, side_ref),
             )
         )
     ]
@@ -76,17 +99,11 @@
 
     barrier = pltpu.get_barrier_semaphore()
 
-    def greet(i, carry):
-        there = lax.rem(me + i, n)
-        pl.semaphore_signal(
-            barrier,
-            inc=1,
-            device_id={"blocks": lax.div(there, nl), "lev": lax.rem(there, nl)},
-            device_id_type=MESH,
+    each_other(
+        lambda slot, device: pl.semaphore_signal(
+            barrier, inc=1, device_id=device, device_id_type=MESH
         )
-        return carry
-
-    lax.fori_loop(1, n, greet, 0)
+    )
 
     lane = lax.broadcasted_iota(jnp.int32, (rows, cols), 1)
     row = lax.broadcasted_iota(jnp.int32, (rows, cols), 0)
@@ -105,6 +122,9 @@
     edge_ref[...] = strip.T
 
     loads[5].wait()
+    loads[7].wait()
+    loads[8].wait()
+    loads[9].wait()
     t_east = edge_ref[pl.ds(0, levels, stride=2), :]
     t_west = edge_ref[pl.ds(1, levels, stride=2), :]
     u_east = edge_ref[pl.ds(2 * levels, levels, stride=2), :]
@@ -116,7 +136,7 @@
     t_edges = (t_west, t_east, t_south, t_north)
     f_edges = (u_west, u_east, v_south, v_north)
     sides = [nbr_ref[0, s] for s in range(4)]
-    fold = fold_ref[0]
+    fold = fold_ref[0, 0]
     blank = jnp.zeros((levels, cols), F32)
 
     def compose(there):
@@ -134,7 +154,7 @@
             pay_ref[i - 1, p * levels : (p + 1) * levels, :] = part
         return carry
 
-    lax.fori_loop(1, nb, pack, 0)
+    lax.fori_loop(1, nb, pack, 0, unroll=unroll)
 
     loads[4].wait()
     last = bottom - 1
@@ -167,20 +187,17 @@
         ).start()
         return carry
 
-    def send_part(i, carry):
-        there = lax.rem(me + i, n)
-        pltpu.make_async_remote_copy(
+    each_other(
+        lambda slot, device: pltpu.make_async_remote_copy(
             src_ref=part_ref,
-            dst_ref=parts_ref.at[i - 1],
+            dst_ref=parts_ref.at[slot],
             send_sem=part_send,
             recv_sem=part_recv,
-            device_id={"blocks": lax.div(there, nl), "lev": lax.rem(there, nl)},
+            device_id=device,
             device_id_type=MESH,
         ).start()
-        return carry
-
-    lax.fori_loop(1, n, send_part, 0)
-    lax.fori_loop(1, nb, send_edges, 0)
+    )
+    lax.fori_loop(1, nb, send_edges, 0, unroll=unroll)
 
     loads[6].wait()
     inverse = 1.0 / shave
@@ -225,7 +242,7 @@
         return found_t, found_f, jnp.where(hit, over_t, fold_t), jnp.where(hit, over_f, fold_f)
 
     found_t, found_f, fold_t, fold_f = lax.fori_loop(
-        1, nb, collect, (found_t, found_f, own[2], own[3])
+        1, nb, collect, (found_t, found_f, own[2], own[3]), unroll=unroll
     )
     mirror = (
         lax.broadcasted_iota(jnp.int32, (cols, cols), 0)
@@ -275,12 +292,6 @@
     struck = jnp.where(shave < THIN_LIMIT, last, -1)
     struck_west = pltpu.roll(struck, 1, 1)
 
-    pltpu.make_async_copy(parts_ref, parts_ref, part_recv).wait()
-    total = lax.fori_loop(0, n - 1, lambda i, carry: carry + parts_ref[i], own_part)
-    total_source = jnp.sum(jnp.where(first_half, total, 0.0), axis=1, keepdims=True)
-    total_volume = jnp.sum(jnp.where(first_half, 0.0, total), axis=1, keepdims=True)
-    mean = total_source / total_volume
-
     for k in range(levels):
         chosen = (place == k) & (place_lane == 0) | (place == levels + k) & (place_lane == cols - 1)
         side_gain = lax.dot_general(
@@ -294,7 +305,18 @@
         merged = weight * x + partner_weight * pltpu.roll(x, cols - 1, 1)
         x = jnp.where(struck == k, merged, x)
         x = jnp.where(struck_west == k, pltpu.roll(merged, 1, 1), x)
-        out_ref[k] = jnp.where(k < bottom, x - mean, 0.0)
+        x_ref[k] = x
+
+    pltpu.make_async_copy(parts_ref, parts_ref, part_recv).wait()
+    total = lax.fori_loop(
+        0, n - 1, lambda i, carry: carry + parts_ref[i], own_part, unroll=unroll
+    )
+    total_source = jnp.sum(jnp.where(first_half, total, 0.0), axis=1, keepdims=True)
+    total_volume = jnp.sum(jnp.where(first_half, 0.0, total), axis=1, keepdims=True)
+    mean = total_source / total_volume
+
+    for k in range(levels):
+        out_ref[k] = jnp.where(k < bottom, x_ref[k] - mean, 0.0)
 
     pltpu.make_async_copy(halo_ref, halo_ref, edge_send).wait()
     pltpu.make_async_copy(parts_ref, parts_ref, part_send).wait()
@@ -316,15 +338,16 @@
     thin_pairs,
 ):
     levels, rows, cols = tracers.shape[2:]
+    in_hbm = functools.partial(pltpu.with_memory_space_constraint, memory_space=pltpu.HBM)
     cube = (levels, rows, cols)
     n = nb * nl
-    smem = pl.BlockSpec(memory_space=pltpu.SMEM)
     vmem = pl.BlockSpec(memory_space=pltpu.VMEM)
+    grant = (12 << 20) + 4 * cols * (8 * levels * nb + 8 * n)
     anywhere = pl.BlockSpec(memory_space=pl.ANY)
     stepped = pl.pallas_call(
         functools.partial(kernel, nb, nl),
-        out_shape=jax.ShapeDtypeStruct(cube, F32),
-        in_specs=[smem, smem, vmem] + [anywhere] * 7,
+        out_shape=pltpu.VMEM(cube, F32),
+        in_specs=[anywhere] * 10,
         out_specs=vmem,
         scratch_shapes=[
             pltpu.VMEM(cube, F32),
@@ -334,30 +357,35 @@
             pltpu.VMEM(cube, F32),
             pltpu.VMEM((rows, cols), jnp.int32),
             pltpu.VMEM((rows, cols), F32),
+            pltpu.SMEM((1, 4), jnp.int32),
+            pltpu.SMEM((1, 1), jnp.int32),
+            pltpu.VMEM((4, cols), jnp.int32),
             pltpu.VMEM(cube, F32),
             pltpu.VMEM((cols, rows), F32),
             pltpu.VMEM((nb - 1, 4 * levels, cols), F32),
             pltpu.VMEM((nb - 1, 4 * levels, cols), F32),
             pltpu.VMEM((1, cols), F32),
             pltpu.VMEM((n - 1, 1, cols), F32),
-            pltpu.SemaphoreType.DMA((7,)),
+            pltpu.SemaphoreType.DMA((10,)),
             pltpu.SemaphoreType.DMA,
             pltpu.SemaphoreType.DMA,
             pltpu.SemaphoreType.DMA,
             pltpu.SemaphoreType.DMA,
         ],
-        compiler_params=pltpu.CompilerParams(collective_id=0, has_side_effects=True),
+        compiler_params=pltpu.CompilerParams(
+            collective_id=0, has_side_effects=True, vmem_limit_bytes=grant
+        ),
     )(
-        neighbors,
-        fold_partner,
-        side_bottom.reshape(4, cols),
-        tracers.reshape(cube),
-        east_velocity.reshape(cube),
-        north_velocity.reshape(cube),
-        upward_velocity.reshape(cube),
-        target.reshape(cube),
-        bottom.reshape(rows, cols),
-        shave_fraction.reshape(rows, cols),
+        in_hbm(neighbors),
+        fold_partner.reshape(1, 1),
+        in_hbm(side_bottom.reshape(4, cols)),
+        in_hbm(tracers.reshape(cube)),
+        in_hbm(east_velocity.reshape(cube)),
+        in_hbm(north_velocity.reshape(cube)),
+        in_hbm(upward_velocity.reshape(cube)),
+        in_hbm(target.reshape(cube)),
+        in_hbm(bottom.reshape(rows, cols)),
+        in_hbm(shave_fraction.reshape(rows, cols)),
     )
     return stepped.reshape(tracers.shape)
 

time: 16.3 us -> 13.4 us (0.82)
  Pallas kernels: 13.6 us -> 11.8 us
  local copies, waits for them, and re-layouts: 1.87 us -> 0.8 us
    pallas_call x1, Pallas kernels: 13.6 us -> 11.8 us  [local(): pl.pallas_call(functools.partial(kernel, nb, nl), out_shape=pltpu.VMEM(cu...]
    unnamed x1, local copies, waits for them, and re-layouts: 1.87 us -> 0.8 us
where the time goes in v2:
time: 13.4 us; the launch traced here: 13.3 us
  Pallas kernels  11.8 us (88%)
  local copies, waits for them, and re-layouts  0.8 us (6%)
  between operations  0.66 us (5%)
    pallas_call x1, Pallas kernels, local(): pl.pallas_call(functools.partial(kernel, nb, nl), out_shape=pltpu.VMEM(cu...  11.8 us
    unnamed x1, local copies, waits for them, and re-layouts  0.8 us

profile of v2, /device:TPU:0, one launch (start us, length us, event | category | flops | bytes accessed | tf_op | source)
XLA Modules:
  0.0 13.3 jit_solution(5197751114366719485)
XLA Ops:
  0.7 11.8 %shard_map.100 = f32[8,128,128]{2,1,0:T(8,128)S(1)} custom-call(s32[1,4]{1,0:T(1,128)} %nbr_hbm.1, s32[1,1]{1,0:T(1,128)} %bitcast.10.fold_hbm, s32[4,128]{1,0:T(4,128)} %bitcast.19, f32[8,128,128]{2,1,0:T(8,128)} %bitcast.12, f32[8,128,128]{2,1,0:T(8,128)} %bitcast.13, f32[8,128,128]{2,1,0:T(8,128)} %bitcast.14, f32[8,128,128]{2,1,0:T(8,128)} %bitcast.15, ...), custom_call_target="tpu_custom_call" | custom-call | tf_op jit(solution)/shard_map/pallas_call | solution.py:347
  12.5 0.8 %copy.12 = f32[1,1,8,128,128]{4,3,2,1,0:T(8,128)} copy(f32[1,1,8,128,128]{4,3,2,1,0:T(8,128)S(1)} %bitcast.11) | data formatting | bytes 1048576

commit v3 on v2

--- a/solution.py
+++ b/solution.py
@@ -46,11 +46,13 @@
     edge_ref,
     pay_ref,
     halo_ref,
-    part_ref,
+    group_ref,
     parts_ref,
     in_sem,
     edge_send,
     edge_recv,
+    group_send,
+    group_recv,
     part_send,
     part_recv,
 ):
@@ -60,22 +62,19 @@
     block = lax.axis_index("blocks")
     lev = lax.axis_index("lev")
 
-    def each_other(visit):
-        def outer(i, carry):
-            there = lax.rem(block + i, nb)
-
-            def inner(j, carry):
-                visit(i * nl + j - 1, {"blocks": there, "lev": lax.rem(lev + j, nl)})
-                return carry
-
-            return lax.fori_loop(0, nl, inner, carry, unroll=unroll)
-
-        def first(j, carry):
-            visit(j - 1, {"blocks": block, "lev": lax.rem(lev + j, nl)})
+    def block_peers(visit):
+        def step(i, carry):
+            visit(i - 1, {"blocks": lax.rem(block + i, nb), "lev": lev})
             return carry
 
-        lax.fori_loop(1, nb, outer, 0, unroll=unroll)
-        lax.fori_loop(1, nl, first, 0, unroll=unroll)
+        lax.fori_loop(1, nb, step, 0, unroll=unroll)
+
+    def lev_peers(visit):
+        def step(i, carry):
+            visit(i - 1, {"blocks": block, "lev": lax.rem(lev + i, nl)})
+            return carry
+
+        lax.fori_loop(1, nl, step, 0, unroll=unroll)
 
     loads = [
         pltpu.make_async_copy(src, dst, in_sem.at[i])
@@ -99,11 +98,11 @@
 
     barrier = pltpu.get_barrier_semaphore()
 
-    each_other(
-        lambda slot, device: pl.semaphore_signal(
-            barrier, inc=1, device_id=device, device_id_type=MESH
-        )
-    )
+    def greet(slot, device):
+        pl.semaphore_signal(barrier, inc=1, device_id=device, device_id_type=MESH)
+
+    block_peers(greet)
+    lev_peers(greet)
 
     lane = lax.broadcasted_iota(jnp.int32, (rows, cols), 1)
     row = lax.broadcasted_iota(jnp.int32, (rows, cols), 0)
@@ -172,32 +171,30 @@
         source + pltpu.roll(source, half, 1),
         volume + pltpu.roll(volume, half, 1),
     )
-    part_ref[...] = own_part
-
-    pl.semaphore_wait(barrier, n - 1)
-
-    def send_edges(i, carry):
+    group_ref[nl - 1] = own_part
+
+    pl.semaphore_wait(barrier, nb + nl - 2)
+
+    def send(src, dst, sems, device):
         pltpu.make_async_remote_copy(
-            src_ref=pay_ref.at[i - 1],
-            dst_ref=halo_ref.at[i - 1],
-            send_sem=edge_send,
-            recv_sem=edge_recv,
-            device_id={"blocks": lax.rem(block + i, nb), "lev": lev},
-            device_id_type=MESH,
-        ).start()
-        return carry
-
-    each_other(
-        lambda slot, device: pltpu.make_async_remote_copy(
-            src_ref=part_ref,
-            dst_ref=parts_ref.at[slot],
-            send_sem=part_send,
-            recv_sem=part_recv,
+            src_ref=src,
+            dst_ref=dst,
+            send_sem=sems[0],
+            recv_sem=sems[1],
             device_id=device,
             device_id_type=MESH,
         ).start()
-    )
-    lax.fori_loop(1, nb, send_edges, 0, unroll=unroll)
+
+    lev_peers(
+        lambda slot, device: send(
+            group_ref.at[nl - 1], group_ref.at[slot], (group_send, group_recv), device
+        )
+    )
+    block_peers(
+        lambda slot, device: send(
+            pay_ref.at[slot], halo_ref.at[slot], (edge_send, edge_recv), device
+        )
+    )
 
     loads[6].wait()
     inverse = 1.0 / shave
@@ -205,7 +202,15 @@
     open_east = jnp.where(lane == cols - 1, 0, jnp.minimum(bottom, bottom_east))
     open_north = jnp.where(row == rows - 1, 0, jnp.minimum(bottom, pltpu.roll(bottom, rows - 1, 0)))
     upper = jnp.zeros((rows, cols), F32)
+    received = group_ref.at[0 : nl - 1]
     for k in range(levels):
+        if k == levels // 2:
+            pltpu.make_async_copy(received, received, group_recv).wait()
+            block_peers(
+                lambda slot, device: send(
+                    group_ref, parts_ref.at[slot], (part_send, part_recv), device
+                )
+            )
         t = t_ref[k]
         u = u_ref[k]
         v = v_ref[k]
@@ -308,8 +313,9 @@
         x_ref[k] = x
 
     pltpu.make_async_copy(parts_ref, parts_ref, part_recv).wait()
+    total = jnp.sum(group_ref[...], axis=0)
     total = lax.fori_loop(
-        0, n - 1, lambda i, carry: carry + parts_ref[i], own_part, unroll=unroll
+        0, nb - 1, lambda i, carry: carry + jnp.sum(parts_ref[i], axis=0), total, unroll=unroll
     )
     total_source = jnp.sum(jnp.where(first_half, total, 0.0), axis=1, keepdims=True)
     total_volume = jnp.sum(jnp.where(first_half, 0.0, total), axis=1, keepdims=True)
@@ -319,6 +325,7 @@
         out_ref[k] = jnp.where(k < bottom, x_ref[k] - mean, 0.0)
 
     pltpu.make_async_copy(halo_ref, halo_ref, edge_send).wait()
+    pltpu.make_async_copy(received, received, group_send).wait()
     pltpu.make_async_copy(parts_ref, parts_ref, part_send).wait()
 
 
@@ -364,9 +371,11 @@
             pltpu.VMEM((cols, rows), F32),
             pltpu.VMEM((nb - 1, 4 * levels, cols), F32),
             pltpu.VMEM((nb - 1, 4 * levels, cols), F32),
-            pltpu.VMEM((1, cols), F32),
-            pltpu.VMEM((n - 1, 1, cols), F32),
+            pltpu.VMEM((nl, 1, cols), F32),
+            pltpu.VMEM((nb - 1, nl, 1, cols), F32),
             pltpu.SemaphoreType.DMA((10,)),
+            pltpu.SemaphoreType.DMA,
+            pltpu.SemaphoreType.DMA,
             pltpu.SemaphoreType.DMA,
             pltpu.SemaphoreType.DMA,
             pltpu.SemaphoreType.DMA,

time: 13.4 us -> 14.7 us (1.097)
  Pallas kernels: 11.8 us -> 13.1 us
    pallas_call x1, Pallas kernels: 11.8 us -> 13.1 us  [local(): pl.pallas_call(functools.partial(kernel, nb, nl), out_shape=pltpu.VMEM(cu...]
where the time goes in v3:
time: 14.7 us; the launch traced here: 14.5 us
  Pallas kernels  13.1 us (89%)
  local copies, waits for them, and re-layouts  0.8 us (5%)
  between operations  0.66 us (4%)
    pallas_call x1, Pallas kernels, local(): pl.pallas_call(functools.partial(kernel, nb, nl), out_shape=pltpu.VMEM(cu...  13.1 us
    unnamed x1, local copies, waits for them, and re-layouts  0.8 us

profile of v3, /device:TPU:0, one launch (start us, length us, event | category | flops | bytes accessed | tf_op | source)
XLA Modules:
  0.0 14.5 jit_solution(10836221990983789824)
XLA Ops:
  0.7 13.1 %shard_map.100 = f32[8,128,128]{2,1,0:T(8,128)S(1)} custom-call(s32[1,4]{1,0:T(1,128)} %nbr_hbm.1, s32[1,1]{1,0:T(1,128)} %bitcast.10.fold_hbm, s32[4,128]{1,0:T(4,128)} %bitcast.19, f32[8,128,128]{2,1,0:T(8,128)} %bitcast.12, f32[8,128,128]{2,1,0:T(8,128)} %bitcast.13, f32[8,128,128]{2,1,0:T(8,128)} %bitcast.14, f32[8,128,128]{2,1,0:T(8,128)} %bitcast.15, ...), custom_call_target="tpu_custom_call" | custom-call | tf_op jit(solution)/shard_map/pallas_call | solution.py:354
  13.7 0.8 %copy.12 = f32[1,1,8,128,128]{4,3,2,1,0:T(8,128)} copy(f32[1,1,8,128,128]{4,3,2,1,0:T(8,128)S(1)} %bitcast.11) | data formatting | bytes 1048576

commit v4 on v3

--- a/solution.py
+++ b/solution.py
@@ -93,8 +93,8 @@
             )
         )
     ]
-    for load in loads:
-        load.start()
+    for i in (7, 8, 9, 2, 3, 0, 1, 5, 4):
+        loads[i].start()
 
     barrier = pltpu.get_barrier_semaphore()
 
@@ -103,6 +103,8 @@
 
     block_peers(greet)
     lev_peers(greet)
+
+    loads[6].start()
 
     lane = lax.broadcasted_iota(jnp.int32, (rows, cols), 1)
     row = lax.broadcasted_iota(jnp.int32, (rows, cols), 0)
@@ -171,7 +173,7 @@
         source + pltpu.roll(source, half, 1),
         volume + pltpu.roll(volume, half, 1),
     )
-    group_ref[nl - 1] = own_part
+    group_ref[nb - 1] = own_part
 
     pl.semaphore_wait(barrier, nb + nl - 2)
 
@@ -185,9 +187,9 @@
             device_id_type=MESH,
         ).start()
 
-    lev_peers(
+    block_peers(
         lambda slot, device: send(
-            group_ref.at[nl - 1], group_ref.at[slot], (group_send, group_recv), device
+            group_ref.at[nb - 1], group_ref.at[slot], (group_send, group_recv), device
         )
     )
     block_peers(
@@ -202,15 +204,7 @@
     open_east = jnp.where(lane == cols - 1, 0, jnp.minimum(bottom, bottom_east))
     open_north = jnp.where(row == rows - 1, 0, jnp.minimum(bottom, pltpu.roll(bottom, rows - 1, 0)))
     upper = jnp.zeros((rows, cols), F32)
-    received = group_ref.at[0 : nl - 1]
     for k in range(levels):
-        if k == levels // 2:
-            pltpu.make_async_copy(received, received, group_recv).wait()
-            block_peers(
-                lambda slot, device: send(
-                    group_ref, parts_ref.at[slot], (part_send, part_recv), device
-                )
-            )
         t = t_ref[k]
         u = u_ref[k]
         v = v_ref[k]
@@ -229,6 +223,11 @@
         upper = lower
         x_ref[k] = t + divergence * jnp.where(k == last, inverse, 1.0) + RATE * (g_ref[k] - t)
 
+    received = group_ref.at[0 : nb - 1]
+    pltpu.make_async_copy(received, received, group_recv).wait()
+    lev_peers(
+        lambda slot, device: send(group_ref, parts_ref.at[slot], (part_send, part_recv), device)
+    )
     pltpu.make_async_copy(halo_ref, halo_ref, edge_recv).wait()
 
     own = compose(block)
@@ -315,7 +314,7 @@
     pltpu.make_async_copy(parts_ref, parts_ref, part_recv).wait()
     total = jnp.sum(group_ref[...], axis=0)
     total = lax.fori_loop(
-        0, nb - 1, lambda i, carry: carry + jnp.sum(parts_ref[i], axis=0), total, unroll=unroll
+        0, nl - 1, lambda i, carry: carry + jnp.sum(parts_ref[i], axis=0), total, unroll=unroll
     )
     total_source = jnp.sum(jnp.where(first_half, total, 0.0), axis=1, keepdims=True)
     total_volume = jnp.sum(jnp.where(first_half, 0.0, total), axis=1, keepdims=True)
@@ -371,8 +370,8 @@
             pltpu.VMEM((cols, rows), F32),
             pltpu.VMEM((nb - 1, 4 * levels, cols), F32),
             pltpu.VMEM((nb - 1, 4 * levels, cols), F32),
-            pltpu.VMEM((nl, 1, cols), F32),
-            pltpu.VMEM((nb - 1, nl, 1, cols), F32),
+            pltpu.VMEM((nb, 1, cols), F32),
+            pltpu.VMEM((nl - 1, nb, 1, cols), F32),
             pltpu.SemaphoreType.DMA((10,)),
             pltpu.SemaphoreType.DMA,
             pltpu.SemaphoreType.DMA,

time: 14.7 us -> 14.8 us (level)
  no operation moved by 1% of the time
where the time goes in v4:
time: 14.8 us; the launch traced here: 14.6 us
  Pallas kernels  13.2 us (89%)
  local copies, waits for them, and re-layouts  0.8 us (5%)
  between operations  0.66 us (4%)
    pallas_call x1, Pallas kernels, local(): pl.pallas_call(functools.partial(kernel, nb, nl), out_shape=pltpu.VMEM(cu...  13.2 us
    unnamed x1, local copies, waits for them, and re-layouts  0.8 us

profile of v4, /device:TPU:0, one launch (start us, length us, event | category | flops | bytes accessed | tf_op | source)
XLA Modules:
  0.0 14.6 jit_solution(17506600762804258739)
XLA Ops:
  0.7 13.2 %shard_map.100 = f32[8,128,128]{2,1,0:T(8,128)S(1)} custom-call(s32[1,4]{1,0:T(1,128)} %nbr_hbm.1, s32[1,1]{1,0:T(1,128)} %bitcast.10.fold_hbm, s32[4,128]{1,0:T(4,128)} %bitcast.19, f32[8,128,128]{2,1,0:T(8,128)} %bitcast.12, f32[8,128,128]{2,1,0:T(8,128)} %bitcast.13, f32[8,128,128]{2,1,0:T(8,128)} %bitcast.14, f32[8,128,128]{2,1,0:T(8,128)} %bitcast.15, ...), custom_call_target="tpu_custom_call" | custom-call | tf_op jit(solution)/shard_map/pallas_call | solution.py:353
  13.8 0.8 %copy.12 = f32[1,1,8,128,128]{4,3,2,1,0:T(8,128)} copy(f32[1,1,8,128,128]{4,3,2,1,0:T(8,128)S(1)} %bitcast.11) | data formatting | bytes 1048576

commit v5 on v2

--- a/solution.py
+++ b/solution.py
@@ -86,16 +86,18 @@
                 (bottom_hbm, bottom_ref),
                 (shave_hbm, shave_ref),
                 (g_hbm, g_ref),
-                (v_hbm, v_ref),
+                (v_hbm.at[:, 8 : rows - 8, :], v_ref.at[:, 8 : rows - 8, :]),
                 (w_hbm, w_ref),
                 (nbr_hbm, nbr_ref),
                 (fold_hbm, fold_ref),
                 (side_hbm, side_ref),
+                (v_hbm.at[:, 0:8, :], v_ref.at[:, 0:8, :]),
+                (v_hbm.at[:, rows - 8 : rows, :], v_ref.at[:, rows - 8 : rows, :]),
             )
         )
     ]
-    for load in loads:
-        load.start()
+    for i in (2, 3, 0, 4, 7, 8, 9, 10, 11, 1, 5, 6):
+        loads[i].start()
 
     barrier = pltpu.get_barrier_semaphore()
 
@@ -109,54 +111,10 @@
     row = lax.broadcasted_iota(jnp.int32, (rows, cols), 0)
     lane_pair = lane // 2
 
-    for load in loads[:4]:
-        load.wait()
+    for i in (2, 3, 0, 4):
+        loads[i].wait()
     bottom = bottom_ref[...]
     shave = shave_ref[...]
-    strip = jnp.zeros((rows, cols), F32)
-    fields = [functools.partial(lambda k: t_ref[k], k) for k in range(levels)]
-    fields += [functools.partial(lambda k: u_ref[k], k) for k in range(levels)]
-    fields += [lambda: bottom.astype(F32), lambda: shave]
-    for j, field in enumerate(fields):
-        strip = jnp.where(lane_pair == j, pltpu.roll(field(), 2 * j + 1, 1), strip)
-    edge_ref[...] = strip.T
-
-    loads[5].wait()
-    loads[7].wait()
-    loads[8].wait()
-    loads[9].wait()
-    t_east = edge_ref[pl.ds(0, levels, stride=2), :]
-    t_west = edge_ref[pl.ds(1, levels, stride=2), :]
-    u_east = edge_ref[pl.ds(2 * levels, levels, stride=2), :]
-    u_west = edge_ref[pl.ds(2 * levels + 1, levels, stride=2), :]
-    t_south = t_ref[:, 0, :]
-    t_north = t_ref[:, rows - 1, :]
-    v_south = v_ref[:, 0, :]
-    v_north = v_ref[:, rows - 1, :]
-    t_edges = (t_west, t_east, t_south, t_north)
-    f_edges = (u_west, u_east, v_south, v_north)
-    sides = [nbr_ref[0, s] for s in range(4)]
-    fold = fold_ref[0, 0]
-    blank = jnp.zeros((levels, cols), F32)
-
-    def compose(there):
-        t_side, f_side = blank, blank
-        for s in range(4):
-            hit = sides[s] == there
-            t_side = jnp.where(hit, t_edges[s], t_side)
-            f_side = jnp.where(hit, f_edges[s], f_side)
-        hit = fold == there
-        return t_side, f_side, jnp.where(hit, t_north, blank), jnp.where(hit, v_north, blank)
-
-    def pack(i, carry):
-        parts = compose(lax.rem(block + i, nb))
-        for p, part in enumerate(parts):
-            pay_ref[i - 1, p * levels : (p + 1) * levels, :] = part
-        return carry
-
-    lax.fori_loop(1, nb, pack, 0, unroll=unroll)
-
-    loads[4].wait()
     last = bottom - 1
     source = jnp.zeros((rows, cols), F32)
     for k in range(levels):
@@ -174,6 +132,48 @@
     )
     part_ref[...] = own_part
 
+    loads[1].wait()
+    strip = jnp.zeros((rows, cols), F32)
+    fields = [functools.partial(lambda k: t_ref[k], k) for k in range(levels)]
+    fields += [functools.partial(lambda k: u_ref[k], k) for k in range(levels)]
+    fields += [lambda: bottom.astype(F32), lambda: shave]
+    for j, field in enumerate(fields):
+        strip = jnp.where(lane_pair == j, pltpu.roll(field(), 2 * j + 1, 1), strip)
+    edge_ref[...] = strip.T
+
+    for i in (7, 8, 9, 10, 11):
+        loads[i].wait()
+    t_east = edge_ref[pl.ds(0, levels, stride=2), :]
+    t_west = edge_ref[pl.ds(1, levels, stride=2), :]
+    u_east = edge_ref[pl.ds(2 * levels, levels, stride=2), :]
+    u_west = edge_ref[pl.ds(2 * levels + 1, levels, stride=2), :]
+    t_south = t_ref[:, 0, :]
+    t_north = t_ref[:, rows - 1, :]
+    v_south = v_ref[:, 0, :]
+    v_north = v_ref[:, rows - 1, :]
+    t_edges = (t_west, t_east, t_south, t_north)
+    f_edges = (u_west, u_east, v_south, v_north)
+    sides = [nbr_ref[0, s] for s in range(4)]
+    fold = fold_ref[0, 0]
+    blank = jnp.zeros((levels, cols), F32)
+
+    def compose(there):
+        t_side, f_side = blank, blank
+        for s in range(4):
+            hit = sides[s] == there
+            t_side = jnp.where(hit, t_edges[s], t_side)
+            f_side = jnp.where(hit, f_edges[s], f_side)
+        hit = fold == there
+        return t_side, f_side, jnp.where(hit, t_north, blank), jnp.where(hit, v_north, blank)
+
+    def pack(i, carry):
+        parts = compose(lax.rem(block + i, nb))
+        for p, part in enumerate(parts):
+            pay_ref[i - 1, p * levels : (p + 1) * levels, :] = part
+        return carry
+
+    lax.fori_loop(1, nb, pack, 0, unroll=unroll)
+
     pl.semaphore_wait(barrier, n - 1)
 
     def send_edges(i, carry):
@@ -199,6 +199,7 @@
     )
     lax.fori_loop(1, nb, send_edges, 0, unroll=unroll)
 
+    loads[5].wait()
     loads[6].wait()
     inverse = 1.0 / shave
     bottom_east = pltpu.roll(bottom, cols - 1, 1)
@@ -366,7 +367,7 @@
             pltpu.VMEM((nb - 1, 4 * levels, cols), F32),
             pltpu.VMEM((1, cols), F32),
             pltpu.VMEM((n - 1, 1, cols), F32),
-            pltpu.SemaphoreType.DMA((10,)),
+            pltpu.SemaphoreType.DMA((12,)),
             pltpu.SemaphoreType.DMA,
             pltpu.SemaphoreType.DMA,
             pltpu.SemaphoreType.DMA,

time: 13.4 us -> 13.4 us (level)
  no operation moved by 1% of the time
where the time goes in v5:
time: 13.4 us; the launch traced here: 13.3 us
  Pallas kernels  11.8 us (88%)
  local copies, waits for them, and re-layouts  0.8 us (6%)
  between operations  0.66 us (5%)
    pallas_call x1, Pallas kernels, local(): pl.pallas_call(functools.partial(kernel, nb, nl), out_shape=pltpu.VMEM(cu...  11.8 us
    unnamed x1, local copies, waits for them, and re-layouts  0.8 us

profile of v5, /device:TPU:0, one launch (start us, length us, event | category | flops | bytes accessed | tf_op | source)
XLA Modules:
  0.0 13.3 jit_solution(3006731793943274521)
XLA Ops:
  0.7 11.8 %shard_map.100 = f32[8,128,128]{2,1,0:T(8,128)S(1)} custom-call(s32[1,4]{1,0:T(1,128)} %nbr_hbm.1, s32[1,1]{1,0:T(1,128)} %bitcast.10.fold_hbm, s32[4,128]{1,0:T(4,128)} %bitcast.19, f32[8,128,128]{2,1,0:T(8,128)} %bitcast.12, f32[8,128,128]{2,1,0:T(8,128)} %bitcast.13, f32[8,128,128]{2,1,0:T(8,128)} %bitcast.14, f32[8,128,128]{2,1,0:T(8,128)} %bitcast.15, ...), custom_call_target="tpu_custom_call" | custom-call | tf_op jit(solution)/shard_map/pallas_call | solution.py:348
  12.5 0.8 %copy.12 = f32[1,1,8,128,128]{4,3,2,1,0:T(8,128)} copy(f32[1,1,8,128,128]{4,3,2,1,0:T(8,128)S(1)} %bitcast.11) | data formatting | bytes 1048576

commit v6 on v5

--- a/solution.py
+++ b/solution.py
@@ -187,6 +187,7 @@
         ).start()
         return carry
 
+    lax.fori_loop(1, nb, send_edges, 0, unroll=unroll)
     each_other(
         lambda slot, device: pltpu.make_async_remote_copy(
             src_ref=part_ref,
@@ -197,7 +198,6 @@
             device_id_type=MESH,
         ).start()
     )
-    lax.fori_loop(1, nb, send_edges, 0, unroll=unroll)
 
     loads[5].wait()
     loads[6].wait()

time: 13.4 us -> 14 us (1.045)
  Pallas kernels: 11.8 us -> 12.4 us
    pallas_call x1, Pallas kernels: 11.8 us -> 12.4 us  [local(): pl.pallas_call(functools.partial(kernel, nb, nl), out_shape=pltpu.VMEM(cu...]
where the time goes in v6:
time: 14 us; the launch traced here: 13.9 us
  Pallas kernels  12.4 us (89%)
  local copies, waits for them, and re-layouts  0.8 us (6%)
  between operations  0.66 us (5%)
    pallas_call x1, Pallas kernels, local(): pl.pallas_call(functools.partial(kernel, nb, nl), out_shape=pltpu.VMEM(cu...  12.4 us
    unnamed x1, local copies, waits for them, and re-layouts  0.8 us

profile of v6, /device:TPU:0, one launch (start us, length us, event | category | flops | bytes accessed | tf_op | source)
XLA Modules:
  0.0 13.9 jit_solution(11020974236358377652)
XLA Ops:
  0.7 12.4 %shard_map.100 = f32[8,128,128]{2,1,0:T(8,128)S(1)} custom-call(s32[1,4]{1,0:T(1,128)} %nbr_hbm.1, s32[1,1]{1,0:T(1,128)} %bitcast.10.fold_hbm, s32[4,128]{1,0:T(4,128)} %bitcast.19, f32[8,128,128]{2,1,0:T(8,128)} %bitcast.12, f32[8,128,128]{2,1,0:T(8,128)} %bitcast.13, f32[8,128,128]{2,1,0:T(8,128)} %bitcast.14, f32[8,128,128]{2,1,0:T(8,128)} %bitcast.15, ...), custom_call_target="tpu_custom_call" | custom-call | tf_op jit(solution)/shard_map/pallas_call | solution.py:348
  13.1 0.8 %copy.12 = f32[1,1,8,128,128]{4,3,2,1,0:T(8,128)} copy(f32[1,1,8,128,128]{4,3,2,1,0:T(8,128)S(1)} %bitcast.11) | data formatting | bytes 1048576
